TPU v7x, 32 devices: a whole 2x2x4 slice. The times are simulated.
32 devices in a mesh: px: 8 (over z, x), py: 4 (over y, core).
Axes of the slice: x: 2, y: 2, z: 4, core: 2. Of those that a mesh axis runs over, the one named last changes fastest.
Arguments:
- particles: float32 [32, 2, 2, 128, 128], P(('px', 'py')), may hold values from -11 to 11
- orientation: int32 [32], P(('px', 'py')), may hold values from 0 to 7
- wedge_index: int32 [32], P(('px', 'py')), may hold values from 0 to 3
- half_set: int32 [32], P(('px', 'py')), may hold values from 0 to 1
- shell_map: int32 [2, 256, 256], P(None, ('px', 'py')), may hold values from 0 to 31, as said below
Outputs:
- half_maps: float32 [2, 2, 2, 256, 256], P(None, None, None, ('px', 'py'))
- fsc: float32 [32], replicated
Inputs may be any that keep to these rules, and one draw needn't show every extreme that they name: `shell_map`: every shell number occurs in every draw.
All inputs are finite; a program needn't handle non-finite values.
Results may differ from a plain program's by a relative error of at most 0.0003.
Values sent between devices are 32-bit elements; how exact they have to be, the bound alone decides.
No kernel may reach another device: no remote copies, remote signals or barrier semaphores. Data moves between devices by JAX's collectives and lax.ppermute only.
A program may use at most 64 MiB of HBM per device.

v0:
```python
import math
import jax
import jax.numpy as jnp
from jax import lax
from jax.sharding import PartitionSpec as P

NSHELL = 32
wedge_rise = (1, 3, 2, 3)
wedge_run = (1, 2, 1, 1)
sign_first = (1.0, -1.0, -1.0, 1.0, 1.0, -1.0, -1.0, 1.0)
sign_second = (1.0, 1.0, -1.0, -1.0, -1.0, -1.0, 1.0, 1.0)
highest = lax.Precision.HIGHEST


def select(lookup, position):
    entries = jnp.array(lookup)
    return jnp.sum(jnp.where(jnp.arange(len(lookup)) == position, entries, jnp.zeros_like(entries)))


def angle_table(sources, targets, extent):
    phases = sources[:, None] * targets[None, :] % extent
    angles = phases.astype(jnp.float32) * (2.0 * math.pi / extent)
    factor = 1.0 / math.sqrt(extent)
    return (jnp.cos(angles) * factor, jnp.sin(angles) * factor)


def coverage(plane_abs, spectral_abs, wedge_id):
    rise_value = select(wedge_rise, wedge_id)
    run_value = select(wedge_run, wedge_id)
    return (plane_abs[:, None] * run_value <= spectral_abs[None, :] * rise_value).astype(
        jnp.float32
    )


def shards(particles, orientation, wedge_index, half_set, shell_map):
    planes = particles.shape[2]
    box_side = particles.shape[3]
    extent = shell_map.shape[2]
    own_rows = shell_map.shape[1]
    plane_abs = jnp.abs((jnp.arange(planes, dtype=jnp.int32) - planes // 2) * (extent // planes))
    spectral = jnp.arange(extent, dtype=jnp.int32)
    spectral_abs = jnp.minimum(spectral, extent - spectral)
    cos_fwd, sin_fwd = angle_table(
        jnp.arange(box_side, dtype=jnp.int32) - box_side // 2, spectral, extent
    )
    totals = jnp.zeros((2, 2, planes, extent, extent), jnp.float32)
    source = particles[0]
    turn_index = orientation[0]
    swapped = turn_index % 2 == 1
    source = jnp.where(turn_index >= 4, jnp.roll(jnp.flip(source, 1), 1, 1), source)
    source = jnp.where(swapped, jnp.swapaxes(source, 2, 3), source)
    sign_outer = select(sign_first, turn_index)
    sign_inner = select(sign_second, turn_index)
    along_cos = jnp.einsum("czab,bk->czak", source, cos_fwd, precision=highest)
    along_sin = jnp.einsum("czab,bk->czak", source, sin_fwd, precision=highest)
    partial_turn = jnp.stack(
        [along_cos[0] + sign_inner * along_sin[1], along_cos[1] - sign_inner * along_sin[0]]
    )
    outer_cos = jnp.einsum("czak,aj->czjk", partial_turn, cos_fwd, precision=highest)
    outer_sin = jnp.einsum("czak,aj->czjk", partial_turn, sin_fwd, precision=highest)
    spectrum = jnp.stack(
        [outer_cos[0] + sign_outer * outer_sin[1], outer_cos[1] - sign_outer * outer_sin[0]]
    )
    covered = coverage(plane_abs, spectral_abs, wedge_index[0])
    covered = jnp.where(swapped, covered[:, None, :], covered[:, :, None])
    half_id = half_set[0]
    current = lax.dynamic_index_in_dim(totals, half_id, 0, False)
    totals = lax.dynamic_update_index_in_dim(totals, current + spectrum * covered, half_id, 0)
    reduced = lax.psum_scatter(totals, ("px", "py"), scatter_dimension=3, tiled=True)
    half_hot = (half_set[:, None] == jnp.arange(2)).astype(jnp.float32)
    wedge_hot = (wedge_index[:, None] == jnp.arange(4)).astype(jnp.float32)
    parity_hot = (orientation[:, None] % 2 == jnp.arange(2)).astype(jnp.float32)
    local_counts = jnp.einsum("ph,pw,pq->hwq", half_hot, wedge_hot, parity_hot, precision=highest)
    class_totals = lax.psum(local_counts, ("px", "py"))
    row_abs = lax.dynamic_slice_in_dim(
        spectral_abs, lax.axis_index(("px", "py")) * own_rows, own_rows
    )
    row_cover = jnp.stack([coverage(plane_abs, row_abs, wedge_id) for wedge_id in range(4)])
    column_cover = jnp.stack([coverage(plane_abs, spectral_abs, wedge_id) for wedge_id in range(4)])
    by_rows = jnp.einsum("hw,wzt->hzt", class_totals[:, :, 0], row_cover, precision=highest)
    by_columns = jnp.einsum("hw,wzk->hzk", class_totals[:, :, 1], column_cover, precision=highest)
    cover = by_rows[:, :, :, None] + by_columns[:, :, None, :]
    average = reduced / jnp.maximum(cover, 1.0)[:, None]
    cross = average[0, 0] * average[1, 0] + average[0, 1] * average[1, 1]
    power_first = average[0, 0] * average[0, 0] + average[0, 1] * average[0, 1]
    power_second = average[1, 0] * average[1, 0] + average[1, 1] * average[1, 1]
    stacked = jnp.stack([cross, power_first, power_second]).reshape(3, -1)
    membership = (shell_map.reshape(-1)[:, None] == jnp.arange(NSHELL)).astype(jnp.float32)
    shell_part = jnp.dot(stacked, membership, precision=highest)
    shell_total = lax.psum(shell_part, ("px", "py"))
    fsc = shell_total[0] / (jnp.sqrt(shell_total[1] * shell_total[2]) + 1e-06)
    n_rows = lax.axis_size("px")
    n_columns = lax.axis_size("py")
    cos_y, sin_y = angle_table(spectral, spectral, extent)
    middle_cos = jnp.einsum("hcztk,kp->hczpt", average, cos_y, precision=highest)
    middle_sin = jnp.einsum("hcztk,kp->hczpt", average, sin_y, precision=highest)
    middle = jnp.stack(
        [middle_cos[:, 0] - middle_sin[:, 1], middle_sin[:, 0] + middle_cos[:, 1]], axis=1
    )
    arrived = lax.all_to_all(
        lax.all_to_all(middle, "px", split_axis=3, concat_axis=4, tiled=True),
        "py",
        split_axis=3,
        concat_axis=4,
        tiled=True,
    )
    x_slot = spectral // own_rows
    x_source = (x_slot % n_rows * n_columns + x_slot // n_rows) * own_rows + spectral % own_rows
    cos_x, sin_x = angle_table(x_source, spectral, extent)
    final_cos = jnp.einsum("hczym,mx->hczyx", arrived, cos_x, precision=highest)
    final_sin = jnp.einsum("hczym,mx->hczyx", arrived, sin_x, precision=highest)
    half_maps = jnp.stack(
        [final_cos[:, 0] - final_sin[:, 1], final_sin[:, 0] + final_cos[:, 1]], axis=1
    )
    return (half_maps, fsc)


def solution(mesh):
    placed = (
        P(("px", "py"), None, None, None, None),
        P(("px", "py")),
        P(("px", "py")),
        P(("px", "py")),
        P(None, ("px", "py"), None),
    )
    return jax.shard_map(
        shards,
        mesh=mesh,
        in_specs=placed,
        out_specs=(P(None, None, None, ("px", "py"), None), P()),
        check_vma=False,
    )
```

profile of v0, /device:TPU:0, one launch (start us, length us, event | category | flops | bytes accessed | tf_op | source)
XLA Modules:
  0.0 240.1 jit_solution(11886774212349079399)
XLA Ops:
  7.9 1.1 copy.50
  9.0 2.0 fusion.38
  11.0 2.0 fusion.42
  13.1 0.7 fusion.77
  13.8 0.7 fusion.13
  14.5 1.5 convolution_bitcast_fusion.1
  16.0 1.5 convolution_bitcast_fusion
  18.1 0.8 fusion.81
  19.0 0.7 broadcast_multiply_fusion.5
  19.7 0.7 broadcast_multiply_fusion.14
  21.2 1.6 fusion.4
  22.8 0.2 broadcast_in_dim.22
  23.0 0.9 copy-done.1
  24.0 1.3 copy-done
  25.6 42.0 %psum.14 = f32[2,4,2]{1,0,2:T(2,128)S(1)} all-reduce(f32[2,4,2]{1,0,2:T(2,128)S(1)} %multiply_bitcast_fusion), channel_id=1, replica_groups=mesh['px'=8,'py'=4] {'px','py'}, use_global_device_ids=true, to_apply=%region_5.6 | all-reduce | flops 16 | bytes 128 | tf_op jit(solution)/shard_map/psum | solution.py:74
  67.6 0.7 broadcast_multiply_fusion.7
  68.2 0.7 broadcast_multiply_fusion.9
  68.9 0.6 broadcast_multiply_fusion.11
  69.5 0.6 broadcast_multiply_fusion.13
  70.2 0.8 broadcast_multiply_fusion.12
  70.9 1.9 broadcast_multiply_fusion.10
  73.3 0.6 broadcast_multiply_fusion
  73.9 0.6 broadcast_multiply_fusion.1
  74.6 0.7 broadcast_multiply_fusion.2
  75.2 0.7 broadcast_multiply_fusion.3
  76.2 0.1 fusion.68
  76.5 89.9 %reduce-scatter.2.cloned.1.call-done = f32[2,2,2,8,256]{4,3,2,1,0:T(8,128)} async-done(((f32[2,2,2,256,256]{4,3,2,1,0:T(8,128)}), f32[2,2,2,8,256]{4,3,2,1,0:T(8,128)}) %reduce-scatter.2.cloned.1.call-update) | async-done | bytes 65552 | tf_op jit(solution)/shard_map/reduce_scatter | solution.py:69
  166.4 0.8 broadcast_divide_fusion
  167.3 1.3 convolution_bitcast_fusion.2
  168.6 1.3 convolution_bitcast_fusion.3
  170.0 0.7 copy.55
  170.7 2.2 reshape.771
  173.0 3.4 %all-to-all-start = ((f32[8,1,2048]{2,1,0:T(1,128)}), f32[8,1,2048]{2,1,0:T(1,128)S(1)}, u32[]{:S(2)}, u32[]{:S(2)}) async-start(f32[8,1,2048]{2,1,0:T(1,128)} %reshape.771), calls=%async_computation.1 | async-start | bytes 131072 | tf_op jit(solution)/shard_map/all_to_all | solution.py:101
  176.3 0.4 fusion.5
  176.7 39.8 %psum.15 = f32[3,32]{1,0:T(4,128)S(1)} all-reduce(f32[3,32]{1,0:T(4,128)S(1)} %fusion.5), channel_id=1, replica_groups=mesh['px'=8,'py'=4] {'px','py'}, use_global_device_ids=true, to_apply=%region_22.23 | all-reduce | flops 96 | bytes 768 | tf_op jit(solution)/shard_map/psum | solution.py:90
  216.6 0.6 broadcast.865
  217.2 0.8 reduce
  218.0 1.6 reshape.772
  219.6 0.6 copy.56
  220.2 0.2 copy.57
  220.3 0.8 reshape.773
  221.1 3.5 %all-to-all-start.1 = ((f32[4,1,4096]{2,1,0:T(1,128)}), f32[4,1,4096]{2,1,0:T(1,128)S(1)}, u32[]{:S(2)}, u32[]{:S(2)}) async-start(f32[4,1,4096]{2,1,0:T(1,128)} %reshape.773), calls=%async_computation.2 | async-start | bytes 131072 | tf_op jit(solution)/shard_map/all_to_all | solution.py:100
  224.7 0.5 fusion.91
  225.2 3.6 %all-to-all-done.1 = f32[4,1,4096]{2,1,0:T(1,128)S(1)} async-done(((f32[4,1,4096]{2,1,0:T(1,128)}), f32[4,1,4096]{2,1,0:T(1,128)S(1)}, u32[]{:S(2)}, u32[]{:S(2)}) %all-to-all-start.1) | async-done | bytes 65568 | tf_op jit(solution)/shard_map/all_to_all | solution.py:100
  228.8 0.9 reduce.1
  230.0 1.3 fusion.14
  231.3 1.3 fusion.16
  232.6 0.6 pad_maximum_fusion.4
  (50 shorter events, 1.8 us)
Async XLA Ops:
  7.2 5.9 %copy-start.3 = (f32[8]{0:T(128)S(1)}, f32[8]{0:T(128)}, u32[]{:S(2)}) copy-start(f32[8]{0:T(128)} %constant.153.clone) | copy-start | bytes 100
  7.2 5.9 %copy-start.4 = (f32[8]{0:T(128)S(1)}, f32[8]{0:T(128)}, u32[]{:S(2)}) copy-start(f32[8]{0:T(128)} %constant.154.clone) | copy-start | bytes 100
  7.2 159.2 %reduce-scatter.2.cloned.1.call-start = ((), (), s32[]{:S(2)}) async-start(), calls=%async_computation.3 | async-start | bytes 2162688 | tf_op jit(solution)/shard_map/reduce_scatter | solution.py:69
  13.8 4.3 %copy-start.5 = (s32[4]{0:T(128)S(1)}, s32[4]{0:T(128)}, u32[]{:S(2)}) copy-start(s32[4]{0:T(128)} %constant.155.clone) | copy-start | bytes 52
  13.8 4.3 %copy-start.6 = (s32[4]{0:T(128)S(1)}, s32[4]{0:T(128)}, u32[]{:S(2)}) copy-start(s32[4]{0:T(128)} %constant.156.clone) | copy-start | bytes 52
  22.8 1.0 copy-start.1
  23.9 52.5 %copy-start.2 = (s32[2,8,256]{2,1,0:T(8,128)S(1)}, s32[2,8,256]{2,1,0:T(8,128)}, u32[]{:S(2)}) copy-start(s32[2,8,256]{2,1,0:T(8,128)} %param.29) | copy-start | bytes 49156
  24.0 1.4 copy-start
  173.0 43.6 %all-to-all-start = ((f32[8,1,2048]{2,1,0:T(1,128)}), f32[8,1,2048]{2,1,0:T(1,128)S(1)}, u32[]{:S(2)}, u32[]{:S(2)}) async-start(f32[8,1,2048]{2,1,0:T(1,128)} %reshape.771), calls=%async_computation.1 | async-start | bytes 131072 | tf_op jit(solution)/shard_map/all_to_all | solution.py:101
  221.1 7.7 %all-to-all-start.1 = ((f32[4,1,4096]{2,1,0:T(1,128)}), f32[4,1,4096]{2,1,0:T(1,128)S(1)}, u32[]{:S(2)}, u32[]{:S(2)}) async-start(f32[4,1,4096]{2,1,0:T(1,128)} %reshape.773), calls=%async_computation.2 | async-start | bytes 131072 | tf_op jit(solution)/shard_map/all_to_all | solution.py:100
Sparse Core Ops, SparseCore 0:
  25.5 140.9 reduce-scatter.1
where the time goes:
time: 241 us; the launch traced here: 240 us
  waiting for transfers between devices  93.5 us (39%)
  blocking collectives  81.8 us (34%)
  other arithmetic  18 us (7%)
  between operations  16.4 us (7%)
  matrix products  12.8 us (5%)
  local copies, waits for them, and re-layouts  10.6 us (4%)
  starting transfers between devices  6.93 us (3%)
    reduce_scatter x1, waiting for transfers between devices, shards(): lax.psum_scatter(totals, ('px', 'py'), scatter_dimension=3, tiled=True)  89.9 us
    psum x1, blocking collectives, shards(): class_totals = lax.psum(local_counts, ('px', 'py'))  42 us
    psum x1, blocking collectives, shards(): shell_total = lax.psum(shell_part, ('px', 'py'))  39.8 us
    unnamed x22, local copies, waits for them, and re-layouts  7.03 us
    mul x7, other arithmetic, coverage(): spectral_abs[None, :] * rise_value  6 us
  transfers between devices with their start and end apart: 3, of which 2 were waited for; matrix products, arithmetic and copies ran while one was open for 4% of the time, Pallas kernels for 0%

commit v1 on v0

--- a/solution.py
+++ b/solution.py
@@ -87,7 +87,9 @@
     stacked = jnp.stack([cross, power_first, power_second]).reshape(3, -1)
     membership = (shell_map.reshape(-1)[:, None] == jnp.arange(NSHELL)).astype(jnp.float32)
     shell_part = jnp.dot(stacked, membership, precision=highest)
-    shell_total = lax.psum(shell_part, ("px", "py"))
+    shell_total = shell_part
+    for over in ("py", "px"):
+        shell_total = lax.psum(shell_total, over)
     fsc = shell_total[0] / (jnp.sqrt(shell_total[1] * shell_total[2]) + 1e-06)
     n_rows = lax.axis_size("px")
     n_columns = lax.axis_size("py")

time: 241 us -> 228 us (0.946)
  blocking collectives: 81.8 us -> 69.7 us
    psum x1 -> x2, blocking collectives: 39.8 us -> 27.7 us  [shards(): shell_total = lax.psum(shell_total, over)]
where the time goes in v1:
time: 228 us
  waiting for transfers between devices  93.5 us (41%)
  blocking collectives  69.7 us (31%)
  other arithmetic  18 us (8%)
  between operations  16.4 us (7%)
  matrix products  12.8 us (6%)
  local copies, waits for them, and re-layouts  10.6 us (5%)
  starting transfers between devices  6.67 us (3%)
    reduce_scatter x1, waiting for transfers between devices, shards(): lax.psum_scatter(totals, ('px', 'py'), scatter_dimension=3, tiled=True)  89.9 us
    psum x1, blocking collectives, shards(): class_totals = lax.psum(local_counts, ('px', 'py'))  42 us
    psum x2, blocking collectives, shards(): shell_total = lax.psum(shell_total, over)  27.7 us
    unnamed x22, local copies, waits for them, and re-layouts  7.03 us
    mul x7, other arithmetic, coverage(): spectral_abs[None, :] * rise_value  6 us
  transfers between devices with their start and end apart: 3, of which 2 were waited for; matrix products, arithmetic and copies ran while one was open for 4% of the time, Pallas kernels for 0%

profile of v1, /device:TPU:0, one launch (start us, length us, event | category | flops | bytes accessed | tf_op | source)
XLA Modules:
  0.0 227.7 jit_solution(15744842792918333681)
XLA Ops:
  7.9 1.1 copy.50
  9.0 2.0 fusion.38
  11.0 2.0 fusion.42
  13.1 0.7 fusion.77
  13.8 0.7 fusion.13
  14.5 1.5 convolution_bitcast_fusion.1
  16.0 1.5 convolution_bitcast_fusion
  18.1 0.8 fusion.81
  19.0 0.7 broadcast_multiply_fusion.5
  19.7 0.7 broadcast_multiply_fusion.14
  21.2 1.6 fusion.4
  22.8 0.2 broadcast_in_dim.22
  23.0 0.9 copy-done.1
  24.0 1.3 copy-done
  25.6 42.0 %psum.21 = f32[2,4,2]{1,0,2:T(2,128)S(1)} all-reduce(f32[2,4,2]{1,0,2:T(2,128)S(1)} %multiply_bitcast_fusion), channel_id=1, replica_groups=mesh['px'=8,'py'=4] {'px','py'}, use_global_device_ids=true, to_apply=%region_5.6 | all-reduce | flops 16 | bytes 128 | tf_op jit(solution)/shard_map/psum | solution.py:74
  67.6 0.7 broadcast_multiply_fusion.7
  68.2 0.7 broadcast_multiply_fusion.9
  68.9 0.6 broadcast_multiply_fusion.11
  69.5 0.6 broadcast_multiply_fusion.13
  70.2 0.8 broadcast_multiply_fusion.12
  70.9 1.9 broadcast_multiply_fusion.10
  73.3 0.6 broadcast_multiply_fusion
  73.9 0.6 broadcast_multiply_fusion.1
  74.6 0.7 broadcast_multiply_fusion.2
  75.2 0.7 broadcast_multiply_fusion.3
  76.5 89.9 %reduce-scatter.2.cloned.1.call-done = f32[2,2,2,8,256]{4,3,2,1,0:T(8,128)} async-done(((f32[2,2,2,256,256]{4,3,2,1,0:T(8,128)}), f32[2,2,2,8,256]{4,3,2,1,0:T(8,128)}) %reduce-scatter.2.cloned.1.call-update) | async-done | bytes 65552 | tf_op jit(solution)/shard_map/reduce_scatter | solution.py:69
  166.4 0.8 broadcast_divide_fusion
  167.3 1.3 convolution_bitcast_fusion.2
  168.6 1.3 convolution_bitcast_fusion.3
  170.0 0.7 copy.55
  170.7 2.2 reshape.771
  173.0 3.4 %all-to-all-start = ((f32[8,1,2048]{2,1,0:T(1,128)}), f32[8,1,2048]{2,1,0:T(1,128)S(1)}, u32[]{:S(2)}, u32[]{:S(2)}) async-start(f32[8,1,2048]{2,1,0:T(1,128)} %reshape.771), calls=%async_computation.1 | async-start | bytes 131072 | tf_op jit(solution)/shard_map/all_to_all | solution.py:103
  176.3 0.4 fusion.5
  176.7 5.8 %psum.22 = f32[3,32]{1,0:T(4,128)S(1)} all-reduce(f32[3,32]{1,0:T(4,128)S(1)} %fusion.5), channel_id=1, replica_groups=mesh['px'=8,'py'=4] {'py'}, use_global_device_ids=true, to_apply=%region_22.23 | all-reduce | flops 96 | bytes 768 | tf_op jit(solution)/shard_map/psum | solution.py:92
  182.5 21.9 %psum.23 = f32[3,32]{1,0:T(4,128)S(1)} all-reduce(f32[3,32]{1,0:T(4,128)S(1)} %psum.22), channel_id=1, replica_groups=mesh['px'=8,'py'=4] {'px'}, use_global_device_ids=true, to_apply=%region_23.24 | all-reduce | flops 96 | bytes 768 | tf_op jit(solution)/shard_map/psum | solution.py:92
  204.4 0.6 broadcast.865
  205.0 0.8 reduce
  205.8 1.6 reshape.772
  207.4 0.6 copy.56
  208.0 0.2 copy.57
  208.2 0.8 reshape.773
  209.0 3.3 %all-to-all-start.1 = ((f32[4,1,4096]{2,1,0:T(1,128)}), f32[4,1,4096]{2,1,0:T(1,128)S(1)}, u32[]{:S(2)}, u32[]{:S(2)}) async-start(f32[4,1,4096]{2,1,0:T(1,128)} %reshape.773), calls=%async_computation.2 | async-start | bytes 131072 | tf_op jit(solution)/shard_map/all_to_all | solution.py:102
  212.3 0.5 fusion.91
  212.8 3.6 %all-to-all-done.1 = f32[4,1,4096]{2,1,0:T(1,128)S(1)} async-done(((f32[4,1,4096]{2,1,0:T(1,128)}), f32[4,1,4096]{2,1,0:T(1,128)S(1)}, u32[]{:S(2)}, u32[]{:S(2)}) %all-to-all-start.1) | async-done | bytes 65568 | tf_op jit(solution)/shard_map/all_to_all | solution.py:102
  216.3 0.9 reduce.1
  217.6 1.3 fusion.14
  218.9 1.3 fusion.16
  220.2 0.6 pad_maximum_fusion.4
  (51 shorter events, 2.0 us)
Async XLA Ops:
  7.2 5.9 %copy-start.3 = (f32[8]{0:T(128)S(1)}, f32[8]{0:T(128)}, u32[]{:S(2)}) copy-start(f32[8]{0:T(128)} %constant.153.clone) | copy-start | bytes 100
  7.2 5.9 %copy-start.4 = (f32[8]{0:T(128)S(1)}, f32[8]{0:T(128)}, u32[]{:S(2)}) copy-start(f32[8]{0:T(128)} %constant.154.clone) | copy-start | bytes 100
  7.2 159.2 %reduce-scatter.2.cloned.1.call-start = ((), (), s32[]{:S(2)}) async-start(), calls=%async_computation.3 | async-start | bytes 2162688 | tf_op jit(solution)/shard_map/reduce_scatter | solution.py:69
  13.8 4.3 %copy-start.5 = (s32[4]{0:T(128)S(1)}, s32[4]{0:T(128)}, u32[]{:S(2)}) copy-start(s32[4]{0:T(128)} %constant.155.clone) | copy-start | bytes 52
  13.8 4.3 %copy-start.6 = (s32[4]{0:T(128)S(1)}, s32[4]{0:T(128)}, u32[]{:S(2)}) copy-start(s32[4]{0:T(128)} %constant.156.clone) | copy-start | bytes 52
  22.8 1.0 copy-start.1
  23.9 52.5 %copy-start.2 = (s32[2,8,256]{2,1,0:T(8,128)S(1)}, s32[2,8,256]{2,1,0:T(8,128)}, u32[]{:S(2)}) copy-start(s32[2,8,256]{2,1,0:T(8,128)} %param.29) | copy-start | bytes 49156
  24.0 1.4 copy-start
  173.0 31.4 %all-to-all-start = ((f32[8,1,2048]{2,1,0:T(1,128)}), f32[8,1,2048]{2,1,0:T(1,128)S(1)}, u32[]{:S(2)}, u32[]{:S(2)}) async-start(f32[8,1,2048]{2,1,0:T(1,128)} %reshape.771), calls=%async_computation.1 | async-start | bytes 131072 | tf_op jit(solution)/shard_map/all_to_all | solution.py:103
  209.0 7.4 %all-to-all-start.1 = ((f32[4,1,4096]{2,1,0:T(1,128)}), f32[4,1,4096]{2,1,0:T(1,128)S(1)}, u32[]{:S(2)}, u32[]{:S(2)}) async-start(f32[4,1,4096]{2,1,0:T(1,128)} %reshape.773), calls=%async_computation.2 | async-start | bytes 131072 | tf_op jit(solution)/shard_map/all_to_all | solution.py:102
Sparse Core Ops, SparseCore 0:
  25.5 140.9 reduce-scatter.1
